TPU v7x, 32 devices: a whole 2x2x4 slice. The times are simulated.
32 devices in a mesh: seq: 8 (over z, core), head: 4 (over y, x).
Axes of the slice: x: 2, y: 2, z: 4, core: 2. Of those that a mesh axis runs over, the one named last changes fastest.
Arguments:
- inputs: float32 [8192, 5120], P(('seq', 'head')), may hold values from -6 to 6
- log_decay: float32 [8192, 80], P(('seq', 'head')), may hold values from -1 to 0
- input_map: float32 [8192, 128], P(('seq', 'head')), may hold values from -0.31533617 to 0.31533617
- output_map: float32 [8192, 128], P(('seq', 'head')), may hold values from -0.31533617 to 0.31533617
- skip_gain: float32 [80], replicated, may hold values from 0.5 to 2
Outputs:
- outputs: float32 [8192, 5120], P(('seq', 'head'))
All inputs are finite; a program needn't handle non-finite values.
Results may differ from a plain program's by a relative error of at most 0.0001.
Values sent between devices are 32-bit elements; how exact they have to be, the bound alone decides.
A program may use at most 128 MiB of HBM per device.

v0:
```python
import jax
import jax.numpy as jnp
from jax import lax
from jax.sharding import PartitionSpec as P

BLOCK = 128


PRECISE = lax.Precision.HIGHEST


def from_behind(value, axis, steps):
    count = lax.axis_size(axis)
    leading, last = (max(0, -steps), min(count, count - steps))
    return lax.ppermute(value, axis, [(source, source + steps) for source in range(leading, last)])


def scan_blocks(inputs, log_decay, input_map, output_map, head_dim):
    token_count = inputs.shape[0]
    width = inputs.shape[1]
    head_count = log_decay.shape[1]
    state_width = input_map.shape[1]
    blocks = token_count // BLOCK
    x_all = inputs.reshape(blocks, BLOCK, width)
    d_all = log_decay.reshape(blocks, BLOCK, head_count)
    b_all = input_map.reshape(blocks, BLOCK, state_width)
    c_all = output_map.reshape(blocks, BLOCK, state_width)
    running = jnp.cumsum(d_all, axis=1)
    run_heads = jnp.moveaxis(running, 2, 1)
    positions = jnp.arange(BLOCK)
    causal = positions[:, None] >= positions[None, :]
    spread = run_heads[:, :, :, None] - run_heads[:, :, None, :]
    decays = jnp.where(causal[None, None], jnp.exp(jnp.minimum(spread, 0.0)), 0.0)
    scores = jnp.einsum("bin,bjn->bij", c_all, b_all, precision=PRECISE)
    weighted = scores[:, None] * decays
    per_head = x_all.reshape(blocks, BLOCK, head_count, head_dim)
    within = jnp.einsum("bhij,bjhp->bihp", weighted, per_head, precision=PRECISE).reshape(
        blocks, BLOCK, width
    )
    closing = running[:, -1, :]
    remains = jnp.repeat(jnp.exp(closing[:, None, :] - running), head_dim, axis=2)
    own_state = jnp.einsum("bln,blw->bnw", b_all, x_all * remains, precision=PRECISE)
    totals = jnp.cumsum(closing, axis=0)
    before_total = totals - closing
    order = jnp.arange(blocks)
    earlier = order[:, None] > order[None, :]
    gap = before_total[:, None, :] - totals[None, :, :]
    link = jnp.where(earlier[:, :, None], jnp.exp(jnp.minimum(gap, 0.0)), 0.0)
    link_wide = jnp.repeat(link, head_dim, axis=2)
    entering = jnp.einsum("kjw,jnw->knw", link_wide, own_state, precision=PRECISE)
    final_weight = jnp.repeat(jnp.exp(totals[-1][None, :] - totals), head_dim, axis=1)
    memory = jnp.einsum("jw,jnw->nw", final_weight, own_state, precision=PRECISE)
    growth = jnp.repeat(jnp.exp(running), head_dim, axis=2)
    carried = jnp.einsum("bin,bnw->biw", c_all, entering, precision=PRECISE) * growth
    prefix = running + before_total[:, None, :]
    return (
        (within + carried).reshape(token_count, width),
        prefix.reshape(token_count, head_count),
        memory,
        totals[-1],
    )


def shard_chain(summed, memory, head_dim):
    factor = jnp.repeat(jnp.exp(summed), head_dim)[None, :]

    def advance(turn, incoming):
        return from_behind(factor * incoming + memory, "seq", 1)

    return lax.fori_loop(0, lax.axis_size("seq") - 1, advance, jnp.zeros_like(memory))


def on_device(inputs, log_decay, input_map, output_map, skip_gain):
    head_count = skip_gain.shape[0]
    head_dim = inputs.shape[1] // head_count
    state_width = input_map.shape[1]
    groups = lax.axis_size("head")
    local_heads = head_count // groups
    local_width = local_heads * head_dim
    results, prefix, memory, summed = scan_blocks(
        inputs, log_decay, input_map, output_map, head_dim
    )
    got_sum, got_state = (
        lax.all_to_all(
            summed.reshape(1, groups, local_heads), "head", split_axis=1, concat_axis=1, tiled=True
        ),
        lax.all_to_all(
            memory.reshape(state_width, groups, local_width),
            "head",
            split_axis=1,
            concat_axis=1,
            tiled=True,
        ),
    )

    def within_shard(carry, item):
        total_decay, total_state = carry
        decay_here, state_here = item
        scale_now = jnp.repeat(jnp.exp(decay_here), head_dim)[None, :]
        return ((total_decay + decay_here, scale_now * total_state + state_here), carry)

    start_carry = (
        jnp.zeros((local_heads,), jnp.float32),
        jnp.zeros((state_width, local_width), jnp.float32),
    )
    (shard_decay, shard_state), (before_decay, before_state) = lax.scan(
        within_shard, start_carry, (got_sum[0], jnp.moveaxis(got_state, 1, 0))
    )
    incoming = shard_chain(shard_decay, shard_state, head_dim)
    per_source = (
        jnp.repeat(jnp.exp(before_decay), head_dim, axis=1)[:, None, :] * incoming[None]
        + before_state
    )
    back = lax.all_to_all(
        jnp.moveaxis(per_source, 0, 1), "head", split_axis=1, concat_axis=1, tiled=True
    )
    arrived = back.reshape(state_width, head_count * head_dim)
    returned = results + jnp.dot(output_map, arrived, precision=PRECISE) * jnp.repeat(
        jnp.exp(prefix), head_dim, axis=1
    )
    return returned + inputs * jnp.repeat(skip_gain, head_dim)[None, :]


def solution(mesh):
    in_specs = (
        P(("seq", "head"), None),
        P(("seq", "head"), None),
        P(("seq", "head"), None),
        P(("seq", "head"), None),
        P(),
    )
    out_specs = P(("seq", "head"), None)
    return jax.shard_map(
        on_device, mesh=mesh, in_specs=in_specs, out_specs=out_specs, check_vma=False
    )
```

profile of v0, /device:TPU:26, one launch (start us, length us, event | category | flops | bytes accessed | tf_op | source)
XLA Modules:
  0.0 314.4 jit_solution(636426769772568378)
XLA Ops:
  2.0 4.2 %all-to-all-start = ((f32[1,4,20]{2,0,1:T(1,128)}), f32[1,4,20]{2,0,1:T(1,128)S(1)}, u32[]{:S(2)}, u32[]{:S(2)}) async-start(f32[1,4,20]{2,0,1:T(1,128)} %bitcast.17), calls=%async_computation | async-start | bytes 4096 | tf_op jit(solution)/shard_map/all_to_all | solution.py:84
  6.3 5.9 %copy.40 = f32[2,128,5120]{1,2,0:T(8,128)} copy(f32[2,128,5120]{2,1,0:T(8,128)} %bitcast.78) | data formatting | bytes 10485760 | tf_op jit(solution)/shard_map/reshape | solution.py:24
  12.4 2.9 bitcast_multiply_fusion
  15.3 5.2 %convolution_bitcast_fusion.2 = f32[2,128,5120]{1,2,0:T(8,128)S(1)} fusion(f32[2,128,5120]{1,2,0:T(8,128)S(1)} %bitcast_multiply_fusion, f32[2,128,128]{2,1,0:T(8,128)S(1)} %bitcast.93), kind=kOutput, calls=%fused_computation.26 | convolution fusion | flops 2013265920 | bytes 10616832 | tf_op jit(solution)/shard_map/bln,blw->bnw/dot_general | solution.py:42
  20.7 2.2 copy-done.2
  22.9 50.3 %fusion.24 = f32[5120,1,128]{2,1,0:T(1,128)} fusion(f32[2,5120,1]{0,2,1:T(1,128)S(1)} %bitcast.89, f32[2,128,5120]{1,2,0:T(8,128)S(1)} %convolution_bitcast_fusion.2), kind=kOutput, calls=%fused_computation.34 | convolution fusion | flops 15728640 | bytes 7905280 | tf_op jit(solution)/shard_map/jw,jnw->nw/dot_general | solution.py:52
  73.2 4.6 %all-to-all-start.1 = ((f32[128,4,1280]{0,2,1:T(8,128)}), f32[128,4,1280]{0,2,1:T(8,128)}, u32[]{:S(2)}, u32[]{:S(2)}) async-start(f32[128,4,1280]{0,2,1:T(8,128)} %bitcast.24), calls=%async_computation.1 | async-start | bytes 5242880 | tf_op jit(solution)/shard_map/all_to_all | solution.py:87
  77.8 8.4 %reshape.93 = f32[2,128,80,64]{3,2,1,0:T(8,128)} reshape(f32[256,5120]{1,0:T(8,128)} %param.9) | data formatting | bytes 10485760 | tf_op jit(solution)/shard_map/reshape;reshape | solution.py:36
  86.1 5.9 %copy.53 = f32[256,5120]{0,1:T(8,128)} copy(f32[256,5120]{1,0:T(8,128)} %param.9) | data formatting | bytes 10485760 | tf_op args[0]
  92.5 24.9 %fusion.6 = f32[2,80,128,64]{2,3,1,0:T(8,128)} fusion(f32[2,128,80,64]{3,2,1,0:T(8,128)} %reshape.93, f32[2,80,128]{2,1,0:T(8,128)S(1)} %copy.35, f32[2,128,128]{2,1,0:T(8,128)S(1)} %fusion.32, pred[128,128]{1,0:T(8,128)(4,1)S(1)} %iota_compare_fusion), kind=kOutput, calls=%fused_computation.12 | convolution fusion | flops 2023751680 | bytes 10715136 | tf_op jit(solution)/shard_map/bhij,bjhp->bihp/dot_general | solution.py:37
  117.4 5.9 %copy.46 = f32[2,128,5120]{2,1,0:T(8,128)} copy(f32[2,128,5120]{1,2,0:T(8,128)} %bitcast.87) | data formatting | bytes 10485760 | tf_op jit(solution)/shard_map/reshape | solution.py:37
  123.4 2.7 broadcast_in_dim.78
  126.1 6.0 %copy.45 = f32[2,128,5120]{2,1,0:T(8,128)} copy(f32[2,128,5120]{1,2,0:T(8,128)} %bitcast.84) | data formatting | bytes 10485760 | tf_op jit(solution)/shard_map/reshape | solution.py:53
  132.9 11.6 %while.29 = (s32[]{:T(128)}, f32[20]{0:T(128)S(1)}, f32[128,1280]{1,0:T(8,128)S(1)}, f32[4,20]{1,0:T(4,128)S(1)}, f32[4,128,1280]{1,2,0:T(8,128)}, /*index=5*/f3...) while((s32[]{:T(128)}, f32[20]{0:T(128)S(1)}, f32[128,1280]{1,0:T(8,128)S(1)}, ...), condition=%wide.region_3.4_spmd.clone, body=%wide.region_2.3_spmd.clone.sunk | while | flops 491563 | bytes 7885568 | solution.py:106
  144.6 84.9 %while.28 = (s32[]{:T(128)}, f32[128,1280]{1,0:T(8,128)S(1)}, f32[128,1280]{1,0:T(8,128)S(1)}, f32[20]{0:T(128)S(1)}, s32[]{:T(128)}) while((s32[]{:T(128)}, f32[128,1280]{1,0:T(8,128)S(1)}, f32[128,1280]{1,0:T(8,128)S(1)}, f32[20]{0:T(128)S(1)}, s32[]{:T(128)}) %tuple.53), condition=%wide.region_5.6_spmd.clone, body=%wide.region_4.5_spmd.clone.sunk | while | flops 327682 | bytes 4608181 | solution.py:70
  146.8 10.0 %collective-permute-done = f32[128,1280]{1,0:T(8,128)S(1)} collective-permute-done((f32[128,1280]{1,0:T(8,128)S(1)}, f32[128,1280]{1,0:T(8,128)S(1)}, u32[]{:S(2)}, u32[]{:S(2)}) %collective-permute-start) | collective-permute-done | bytes 655392 | tf_op jit(solution)/shard_map/while/body/eval_jaxpr/ppermute | solution.py:15
  158.9 10.0 %collective-permute-done = f32[128,1280]{1,0:T(8,128)S(1)} collective-permute-done((f32[128,1280]{1,0:T(8,128)S(1)}, f32[128,1280]{1,0:T(8,128)S(1)}, u32[]{:S(2)}, u32[]{:S(2)}) %collective-permute-start) | collective-permute-done | bytes 655392 | tf_op jit(solution)/shard_map/while/body/eval_jaxpr/ppermute | solution.py:15
  171.0 10.0 %collective-permute-done = f32[128,1280]{1,0:T(8,128)S(1)} collective-permute-done((f32[128,1280]{1,0:T(8,128)S(1)}, f32[128,1280]{1,0:T(8,128)S(1)}, u32[]{:S(2)}, u32[]{:S(2)}) %collective-permute-start) | collective-permute-done | bytes 655392 | tf_op jit(solution)/shard_map/while/body/eval_jaxpr/ppermute | solution.py:15
  181.2 1.9 collective-permute-start
  183.1 10.0 %collective-permute-done = f32[128,1280]{1,0:T(8,128)S(1)} collective-permute-done((f32[128,1280]{1,0:T(8,128)S(1)}, f32[128,1280]{1,0:T(8,128)S(1)}, u32[]{:S(2)}, u32[]{:S(2)}) %collective-permute-start) | collective-permute-done | bytes 655392 | tf_op jit(solution)/shard_map/while/body/eval_jaxpr/ppermute | solution.py:15
  193.3 1.9 collective-permute-start
  195.3 10.0 %collective-permute-done = f32[128,1280]{1,0:T(8,128)S(1)} collective-permute-done((f32[128,1280]{1,0:T(8,128)S(1)}, f32[128,1280]{1,0:T(8,128)S(1)}, u32[]{:S(2)}, u32[]{:S(2)}) %collective-permute-start) | collective-permute-done | bytes 655392 | tf_op jit(solution)/shard_map/while/body/eval_jaxpr/ppermute | solution.py:15
  207.4 10.0 %collective-permute-done = f32[128,1280]{1,0:T(8,128)S(1)} collective-permute-done((f32[128,1280]{1,0:T(8,128)S(1)}, f32[128,1280]{1,0:T(8,128)S(1)}, u32[]{:S(2)}, u32[]{:S(2)}) %collective-permute-start) | collective-permute-done | bytes 655392 | tf_op jit(solution)/shard_map/while/body/eval_jaxpr/ppermute | solution.py:15
  219.5 10.0 %collective-permute-done = f32[128,1280]{1,0:T(8,128)S(1)} collective-permute-done((f32[128,1280]{1,0:T(8,128)S(1)}, f32[128,1280]{1,0:T(8,128)S(1)}, u32[]{:S(2)}, u32[]{:S(2)}) %collective-permute-start) | collective-permute-done | bytes 655392 | tf_op jit(solution)/shard_map/while/body/eval_jaxpr/ppermute | solution.py:15
  229.9 3.2 %add_bitcast_fusion = f32[128,4,1280]{0,2,1:T(8,128)} fusion(f32[4,128,1280]{1,2,0:T(8,128)} %get-tuple-element.71, f32[128,1280]{0,1:T(8,128)S(1)} %copy.49, f32[4,1280]{1,0:T(4,128)S(1)} %mul.66), kind=kLoop, calls=%fused_computation.39 | loop fusion | flops 1310720 | bytes 5918720 | tf_op jit(solution)/shard_map/transpose | solution.py:115
  233.1 4.3 %all-to-all-start.2 = ((f32[128,4,1280]{0,2,1:T(8,128)}), f32[128,4,1280]{0,2,1:T(8,128)S(1)}, u32[]{:S(2)}, u32[]{:S(2)}) async-start(f32[128,4,1280]{0,2,1:T(8,128)} %add_bitcast_fusion), calls=%async_computation.2 | async-start | bytes 5242880 | tf_op jit(solution)/shard_map/all_to_all | solution.py:114
  238.8 45.4 %fusion.28 = f32[2,128,5120]{1,0,2:T(2,128)S(1)} fusion(f32[2,2,5120]{1,0,2:T(2,128)S(1)} %bitcast.88, f32[2,128,5120]{1,2,0:T(8,128)} %copy-done.2), kind=kOutput, calls=%fused_computation.38 | convolution fusion | flops 31457280 | bytes 10567680 | tf_op jit(solution)/shard_map/kjw,jnw->knw/dot_general | solution.py:50
  284.3 7.0 %fusion.17 = f32[2,128,5120]{2,1,0:T(8,128)} fusion(f32[2,128,5120]{2,1,0:T(8,128)S(1)} %bitcast.80, f32[2,128,5120]{2,1,0:T(8,128)S(1)} %bitcast.82, f32[2,128,128]{2,1,0:T(8,128)S(1)} %bitcast.77, f32[2,128,5120]{1,0,2:T(2,128)S(1)} %fusion.28), kind=kOutput, calls=%fused_computation.25 | convolution fusion | flops 2015887360 | bytes 21102592 | tf_op jit(solution)/shard_map/bin,bnw->biw/dot_general | solution.py:54
  291.3 5.9 %copy.52 = f32[256,5120]{0,1:T(8,128)} copy(f32[256,5120]{1,0:T(8,128)} %bitcast.83) | data formatting | bytes 10485760 | tf_op jit(solution)/shard_map/reshape | solution.py:57
  297.9 2.1 copy-done.1
  300.0 8.3 %fusion.15 = f32[256,5120]{0,1:T(8,128)} fusion(f32[256,5120]{0,1:T(8,128)S(1)} %copy-done.1, f32[256,5120]{0,1:T(8,128)S(1)} %bitcast.85, f32[128,5120]{0,1:T(8,128)S(1)} %bitcast.86, f32[256,128]{1,0:T(8,128)S(1)} %copy-done, f32[256,5120]{0,1:T(8,128)} %copy.53, f32[5120]{0:T(1024)S(1)} %mul.71), kind=kOutput, calls=%fused_computation.22 | convolution fusion | flops 2018508800 | bytes 23744512 | tf_op jit(solution)/shard_map/dot_general | solution.py:118
  308.3 5.9 %copy.54 = f32[256,5120]{1,0:T(8,128)} copy(f32[256,5120]{0,1:T(8,128)} %fusion.15) | data formatting | bytes 10485760 | tf_op jit(solution)/shard_map/add | solution.py:121
  (119 shorter events, 28.9 us)
Async XLA Ops:
  0.0 92.2 %copy-start = (f32[256,128]{1,0:T(8,128)S(1)}, f32[256,128]{1,0:T(8,128)}, u32[]{:S(2)}) copy-start(f32[256,128]{1,0:T(8,128)} %param.12) | copy-start | bytes 393220
  2.0 71.2 %all-to-all-start = ((f32[1,4,20]{2,0,1:T(1,128)}), f32[1,4,20]{2,0,1:T(1,128)S(1)}, u32[]{:S(2)}, u32[]{:S(2)}) async-start(f32[1,4,20]{2,0,1:T(1,128)} %bitcast.17), calls=%async_computation | async-start | bytes 4096 | tf_op jit(solution)/shard_map/all_to_all | solution.py:84
  12.4 2.9 copy-start.3
  20.5 2.4 copy-start.2
  73.2 59.7 %all-to-all-start.1 = ((f32[128,4,1280]{0,2,1:T(8,128)}), f32[128,4,1280]{0,2,1:T(8,128)}, u32[]{:S(2)}, u32[]{:S(2)}) async-start(f32[128,4,1280]{0,2,1:T(8,128)} %bitcast.24), calls=%async_computation.1 | async-start | bytes 5242880 | tf_op jit(solution)/shard_map/all_to_all | solution.py:87
  144.8 11.9 %collective-permute-start = (f32[128,1280]{1,0:T(8,128)S(1)}, f32[128,1280]{1,0:T(8,128)S(1)}, u32[]{:S(2)}, u32[]{:S(2)}) collective-permute-start(f32[128,1280]{1,0:T(8,128)S(1)} %multiply_add_fusion.2), channel_id=1, source_target_pairs={{0,4},{4,8},{8,12},{12,16},{16,20},{20,24},{24,28},{1,5},{5,9},{9,... | collective-permute-start | bytes 1966088 | tf_op jit(solution)/shard_map/while/body/eval_jaxpr/ppermute | solution.py:15
  157.0 11.9 %collective-permute-start = (f32[128,1280]{1,0:T(8,128)S(1)}, f32[128,1280]{1,0:T(8,128)S(1)}, u32[]{:S(2)}, u32[]{:S(2)}) collective-permute-start(f32[128,1280]{1,0:T(8,128)S(1)} %multiply_add_fusion.2), channel_id=1, source_target_pairs={{0,4},{4,8},{8,12},{12,16},{16,20},{20,24},{24,28},{1,5},{5,9},{9,... | collective-permute-start | bytes 1966088 | tf_op jit(solution)/shard_map/while/body/eval_jaxpr/ppermute | solution.py:15
  169.1 11.9 %collective-permute-start = (f32[128,1280]{1,0:T(8,128)S(1)}, f32[128,1280]{1,0:T(8,128)S(1)}, u32[]{:S(2)}, u32[]{:S(2)}) collective-permute-start(f32[128,1280]{1,0:T(8,128)S(1)} %multiply_add_fusion.2), channel_id=1, source_target_pairs={{0,4},{4,8},{8,12},{12,16},{16,20},{20,24},{24,28},{1,5},{5,9},{9,... | collective-permute-start | bytes 1966088 | tf_op jit(solution)/shard_map/while/body/eval_jaxpr/ppermute | solution.py:15
  181.2 11.9 %collective-permute-start = (f32[128,1280]{1,0:T(8,128)S(1)}, f32[128,1280]{1,0:T(8,128)S(1)}, u32[]{:S(2)}, u32[]{:S(2)}) collective-permute-start(f32[128,1280]{1,0:T(8,128)S(1)} %multiply_add_fusion.2), channel_id=1, source_target_pairs={{0,4},{4,8},{8,12},{12,16},{16,20},{20,24},{24,28},{1,5},{5,9},{9,... | collective-permute-start | bytes 1966088 | tf_op jit(solution)/shard_map/while/body/eval_jaxpr/ppermute | solution.py:15
  193.3 11.9 %collective-permute-start = (f32[128,1280]{1,0:T(8,128)S(1)}, f32[128,1280]{1,0:T(8,128)S(1)}, u32[]{:S(2)}, u32[]{:S(2)}) collective-permute-start(f32[128,1280]{1,0:T(8,128)S(1)} %multiply_add_fusion.2), channel_id=1, source_target_pairs={{0,4},{4,8},{8,12},{12,16},{16,20},{20,24},{24,28},{1,5},{5,9},{9,... | collective-permute-start | bytes 1966088 | tf_op jit(solution)/shard_map/while/body/eval_jaxpr/ppermute | solution.py:15
  205.5 11.9 %collective-permute-start = (f32[128,1280]{1,0:T(8,128)S(1)}, f32[128,1280]{1,0:T(8,128)S(1)}, u32[]{:S(2)}, u32[]{:S(2)}) collective-permute-start(f32[128,1280]{1,0:T(8,128)S(1)} %multiply_add_fusion.2), channel_id=1, source_target_pairs={{0,4},{4,8},{8,12},{12,16},{16,20},{20,24},{24,28},{1,5},{5,9},{9,... | collective-permute-start | bytes 1966088 | tf_op jit(solution)/shard_map/while/body/eval_jaxpr/ppermute | solution.py:15
  217.6 11.9 %collective-permute-start = (f32[128,1280]{1,0:T(8,128)S(1)}, f32[128,1280]{1,0:T(8,128)S(1)}, u32[]{:S(2)}, u32[]{:S(2)}) collective-permute-start(f32[128,1280]{1,0:T(8,128)S(1)} %multiply_add_fusion.2), channel_id=1, source_target_pairs={{0,4},{4,8},{8,12},{12,16},{16,20},{20,24},{24,28},{1,5},{5,9},{9,... | collective-permute-start | bytes 1966088 | tf_op jit(solution)/shard_map/while/body/eval_jaxpr/ppermute | solution.py:15
  233.1 4.3 %copy-start.4 = (f32[2,2,80]{1,0,2:T(2,128)S(1)}, f32[2,2,80]{1,0,2:T(2,128)}, u32[]{:S(2)}) copy-start(f32[2,2,80]{1,0,2:T(2,128)} %copy.66) | copy-start | bytes 3844
  233.1 64.3 %all-to-all-start.2 = ((f32[128,4,1280]{0,2,1:T(8,128)}), f32[128,4,1280]{0,2,1:T(8,128)S(1)}, u32[]{:S(2)}, u32[]{:S(2)}) async-start(f32[128,4,1280]{0,2,1:T(8,128)} %add_bitcast_fusion), calls=%async_computation.2 | async-start | bytes 5242880 | tf_op jit(solution)/shard_map/all_to_all | solution.py:114
  237.5 46.8 %slice-start = ((s8[5242880]{0:T(1024)(128)(4,1)}), s8[1048576]{0:T(1024)(128)(4,1)S(1)}, s32[]{:S(2)}) async-start(s8[5242880]{0:T(1024)(128)(4,1)} %bitcast.79), calls=%async_computation.3 | async-start | bytes 2097152
  237.5 46.8 %slice-start.2 = ((s8[5242880]{0:T(1024)(128)(4,1)}), s8[4194304]{0:T(1024)(128)(4,1)S(1)}, s32[]{:S(2)}) async-start(s8[5242880]{0:T(1024)(128)(4,1)} %bitcast.81), calls=%async_computation.5 | async-start | bytes 8388608
  238.8 45.5 %slice-start.1 = ((s8[5242880]{0:T(1024)(128)(4,1)}), s8[4194304]{0:T(1024)(128)(4,1)S(1)}, s32[]{:S(2)}) async-start(s8[5242880]{0:T(1024)(128)(4,1)} %bitcast.79), calls=%async_computation.4 | async-start | bytes 8388608
  238.8 45.5 %slice-start.3 = ((s8[5242880]{0:T(1024)(128)(4,1)}), s8[1048576]{0:T(1024)(128)(4,1)S(1)}, s32[]{:S(2)}) async-start(s8[5242880]{0:T(1024)(128)(4,1)} %bitcast.81), calls=%async_computation.6 | async-start | bytes 2097152
  291.3 6.0 %copy-start.5 = (f32[80]{0:T(128)S(1)}, f32[80]{0:T(128)}, u32[]{:S(2)}) copy-start(f32[80]{0:T(128)} %param.13) | copy-start | bytes 964
  297.5 2.5 copy-start.1
where the time goes:
time: 321 us; the launch traced here: 314 us
  matrix products  142 us (44%)
  waiting for transfers between devices  69.8 us (22%)
  local copies, waits for them, and re-layouts  67.9 us (21%)
  starting transfers between devices  26.6 us (8%)
  other arithmetic  7.84 us (2%)
    ppermute x7, waiting for transfers between devices, from_behind(): lax.ppermute(value, axis, [(source, source + steps) for source in range(l...  69.8 us
    dot_general x1, matrix products, scan_blocks(): jnp.einsum('jw,jnw->nw', final_weight, own_state, precision=PRECISE)  50.3 us
    dot_general x1, matrix products, scan_blocks(): jnp.einsum('kjw,jnw->knw', link_wide, own_state, precision=PRECISE)  45.4 us
    dot_general x1, matrix products, scan_blocks(): jnp.einsum('bhij,bjhp->bihp', weighted, per_head, precision=PRECISE)  24.9 us
    ppermute x7, starting transfers between devices, from_behind(): lax.ppermute(value, axis, [(source, source + steps) for source in range(l...  13.4 us
    unnamed x23, local copies, waits for them, and re-layouts  11 us
    another operation x1, local copies, waits for them, and re-layouts, scan_blocks(): per_head = x_all.reshape(blocks, BLOCK, head_count, head_dim)  8.36 us
    dot_general x1, matrix products, on_device(): jnp.dot(output_map, arrived, precision=PRECISE)  8.34 us
  transfers between devices with their start and end apart: 10, of which 7 were waited for; matrix products, arithmetic and copies ran while one was open for 57% of the time, Pallas kernels for 0%

commit v1 on v0

--- a/solution.py
+++ b/solution.py
@@ -1,6 +1,9 @@
+import functools
 import jax
 import jax.numpy as jnp
 from jax import lax
+from jax.experimental import pallas as pl
+from jax.experimental.pallas import tpu as pltpu
 from jax.sharding import PartitionSpec as P
 
 BLOCK = 128
@@ -121,6 +124,365 @@
     return returned + inputs * jnp.repeat(skip_gain, head_dim)[None, :]
 
 
+MESH = pl.DeviceIdType.MESH
+CHUNK = 256
+LANES = 128
+
+
+def two(value):
+    high = value.astype(jnp.bfloat16)
+    return high, (value - high.astype(jnp.float32)).astype(jnp.bfloat16)
+
+
+def three(value):
+    high = value.astype(jnp.bfloat16)
+    rest = value - high.astype(jnp.float32)
+    middle = rest.astype(jnp.bfloat16)
+    return high, middle, (rest - middle.astype(jnp.float32)).astype(jnp.bfloat16)
+
+
+def left_side(value):
+    high, low = two(value)
+    return jnp.concatenate([high, high, low], axis=1)
+
+
+def right_side(value):
+    high, low = two(value)
+    return jnp.concatenate([high, low, high], axis=0)
+
+
+def mm(a, b):
+    return jnp.dot(a, b, preferred_element_type=jnp.float32)
+
+
+def full_mm(a, b, dims):
+    return lax.dot_general(
+        a, b, (dims, ((), ())), precision=PRECISE, preferred_element_type=jnp.float32
+    )
+
+
+def expander(chunk, depth, heads_per_chunk, head_dim):
+    row = lax.broadcasted_iota(jnp.int32, (depth, CHUNK), 0) & (LANES - 1)
+    column = lax.broadcasted_iota(jnp.int32, (depth, CHUNK), 1) // head_dim
+    hit = row == column + chunk * heads_per_chunk
+    return jnp.where(hit, 1.0, 0.0).astype(jnp.bfloat16)
+
+
+def whole_kernel(
+    groups, shards, head_dim,
+    x_hbm, d_ref, b_ref, c_ref, g_ref, o_hbm,
+    xbuf, obuf, mbuf, rbuf, sbuf, sout, back,
+    first, second, readout, spread, grow, rows,
+    xsem, osem, fsend, frecv, csend, crecv, bsend, brecv,
+):
+    seq = lax.axis_index("seq")
+    me = lax.axis_index("head")
+    chunks = xbuf.shape[0]
+    per = chunks // groups
+    state = b_ref.shape[1]
+    hpc = CHUNK // head_dim
+
+    def x_copy(chunk):
+        columns = pl.ds(pl.multiple_of(chunk * CHUNK, CHUNK), CHUNK)
+        return pltpu.make_async_copy(x_hbm.at[:, columns], xbuf.at[chunk], xsem.at[chunk])
+
+    def o_copy(chunk):
+        columns = pl.ds(pl.multiple_of(chunk * CHUNK, CHUNK), CHUNK)
+        return pltpu.make_async_copy(obuf.at[chunk], o_hbm.at[:, columns], osem.at[chunk])
+
+    def at_turn(turn):
+        k = turn // groups
+        owner = (me + 1 + turn % groups) % groups
+        return k, owner, owner * per + k
+
+    def forth(chunk, k, owner):
+        return pltpu.make_async_remote_copy(
+            src_ref=mbuf.at[chunk],
+            dst_ref=rbuf.at[me * per + k],
+            send_sem=fsend.at[chunk],
+            recv_sem=frecv.at[me * per + k],
+            device_id={"head": owner},
+            device_id_type=MESH,
+        )
+
+    def forth_in(slot):
+        return pltpu.make_async_remote_copy(
+            src_ref=mbuf.at[slot],
+            dst_ref=rbuf.at[slot],
+            send_sem=fsend.at[slot],
+            recv_sem=frecv.at[slot],
+            device_id={"head": (me + 1) % groups},
+            device_id_type=MESH,
+        )
+
+    def chain(k):
+        return pltpu.make_async_remote_copy(
+            src_ref=sout.at[k],
+            dst_ref=sbuf.at[k],
+            send_sem=csend.at[k],
+            recv_sem=crecv.at[k],
+            device_id={"seq": (seq + 1) % shards},
+            device_id_type=MESH,
+        )
+
+    def home(slot, k, target):
+        return pltpu.make_async_remote_copy(
+            src_ref=rbuf.at[slot, pl.ds(0, state)],
+            dst_ref=back.at[me * per + k],
+            send_sem=bsend.at[slot],
+            recv_sem=brecv.at[me * per + k],
+            device_id={"head": target},
+            device_id_type=MESH,
+        )
+
+    def home_in(slot):
+        return pltpu.make_async_remote_copy(
+            src_ref=rbuf.at[slot, pl.ds(0, state)],
+            dst_ref=back.at[slot],
+            send_sem=bsend.at[slot],
+            recv_sem=brecv.at[slot],
+            device_id={"head": (me + 1) % groups},
+            device_id_type=MESH,
+        )
+
+    def load(turn, carry):
+        x_copy(at_turn(turn)[2]).start()
+        return carry
+
+    lax.fori_loop(0, chunks, load, 0)
+
+    barrier = pltpu.get_barrier_semaphore()
+    for step in range(1, groups):
+        pl.semaphore_signal(
+            barrier, inc=1, device_id={"head": (me + step) % groups}, device_id_type=MESH
+        )
+    for step in (1, shards - 1):
+        pl.semaphore_signal(
+            barrier, inc=1, device_id={"seq": (seq + step) % shards}, device_id_type=MESH
+        )
+
+    heads = d_ref.shape[1]
+    below = lax.broadcasted_iota(jnp.int32, (BLOCK, BLOCK), 0)
+    above = lax.broadcasted_iota(jnp.int32, (BLOCK, BLOCK), 1)
+    causal = below >= above
+    ones = jnp.where(causal, 1.0, 0.0).astype(jnp.bfloat16)
+    padding = jnp.zeros((d_ref.shape[0], LANES - heads), jnp.float32)
+    decay = jnp.concatenate([d_ref[...], padding], axis=1)
+    run1 = sum(mm(ones, part) for part in three(decay[:BLOCK]))
+    run2 = sum(mm(ones, part) for part in three(decay[BLOCK:]))
+    end1, end2 = run1[BLOCK - 1 :], run2[BLOCK - 1 :]
+    mid1, mid2 = run1[BLOCK // 2 - 1 : BLOCK // 2], run2[BLOCK // 2 - 1 : BLOCK // 2]
+    total = end1 + end2
+    tables = jnp.concatenate(
+        [
+            jnp.exp(mid1 - run1),
+            jnp.exp(mid2 - run2),
+            jnp.exp(run1 - mid1),
+            jnp.exp(run2 - mid2),
+            jnp.exp(run2 + (end1 - mid1)),
+        ],
+        axis=0,
+    )
+    spread[...] = jnp.concatenate(two(tables), axis=1)
+    grow[...] = jnp.concatenate(
+        two(jnp.concatenate([jnp.exp(run1), jnp.exp(run2 + end1)], axis=0)), axis=1
+    )
+    gain = jnp.concatenate([g_ref[...], jnp.zeros((1, LANES - heads), jnp.float32)], axis=1)
+    line = lax.broadcasted_iota(jnp.int32, (16, LANES), 0)
+    picked = jnp.where(line == 0, jnp.exp(total), 0.0)
+    picked = jnp.where(line == 1, jnp.exp(total - mid1), picked)
+    picked = jnp.where(line == 2, jnp.exp(end2 - mid2), picked)
+    picked = jnp.where(line == 3, gain, picked)
+    rows[...] = jnp.concatenate(three(picked), axis=1)
+
+    b1, b2 = b_ref[:BLOCK], b_ref[BLOCK:]
+    c1, c2 = c_ref[:BLOCK], c_ref[BLOCK:]
+    last = ((1,), (1,))
+    own1 = jnp.where(causal, full_mm(c1, b1, last), 0.0)
+    own2 = jnp.where(causal, full_mm(c2, b2, last), 0.0)
+    cross = full_mm(c2, b1, last)
+    first[...] = left_side(jnp.concatenate([own1, cross, b1.T], axis=0))
+    second[...] = left_side(jnp.concatenate([own2, b2.T], axis=0))
+    readout[...] = left_side(c_ref[...])
+
+    @pl.when(seq == 0)
+    def _():
+        sbuf[...] = jnp.zeros_like(sbuf)
+
+    pl.semaphore_wait(barrier, groups + 1)
+
+    def local(turn, carry):
+        k, owner, chunk = at_turn(turn)
+        x_copy(chunk).wait()
+        x = xbuf[chunk]
+        scale = mm(spread[...], expander(chunk, 2 * LANES, hpc, head_dim))
+        lines = mm(rows[...], expander(chunk, 3 * LANES, hpc, head_dim))
+        weighed = x * scale[: 2 * BLOCK]
+        y1 = mm(first[...], right_side(weighed[:BLOCK]))
+        y2 = mm(second[...], right_side(weighed[BLOCK:]))
+        obuf[chunk, :BLOCK] = y1[:BLOCK] * scale[2 * BLOCK : 3 * BLOCK] + lines[3:4] * x[:BLOCK]
+        obuf[chunk, BLOCK:] = (
+            y2[:BLOCK] * scale[3 * BLOCK : 4 * BLOCK]
+            + y1[BLOCK : 2 * BLOCK] * scale[4 * BLOCK :]
+            + lines[3:4] * x[BLOCK:]
+        )
+        memory = y1[2 * BLOCK :] * lines[1:2] + y2[BLOCK:] * lines[2:3]
+        factor = jnp.broadcast_to(lines[0:1], (8, CHUNK))
+
+        @pl.when(owner == me)
+        def _():
+            rbuf[chunk, :state] = memory
+            rbuf[chunk, state:] = factor
+
+        @pl.when(owner != me)
+        def _():
+            mbuf[chunk, :state] = memory
+            mbuf[chunk, state:] = factor
+            forth(chunk, k, owner).start()
+
+        return carry
+
+    lax.fori_loop(0, chunks, local, 0)
+
+    def link(k, carry):
+        for step in range(1, groups):
+            forth_in(((me + step) % groups) * per + k).wait_recv()
+        factors = [rbuf[j * per + k, state : state + 1] for j in range(groups)]
+        shard = rbuf[k, :state]
+        shard_factor = factors[0]
+        for j in range(1, groups):
+            shard = factors[j] * shard + rbuf[j * per + k, :state]
+            shard_factor = shard_factor * factors[j]
+        sout[k] = shard
+
+        @pl.when(seq > 0)
+        def _():
+            chain(k).wait_recv()
+
+        @pl.when(seq < shards - 1)
+        def _():
+            sout[k] = shard_factor * sbuf[k] + sout[k]
+            chain(k).start()
+
+        incoming = sbuf[k]
+        for j in range(groups):
+            slot = j * per + k
+            here = rbuf[slot, :state]
+            rbuf[slot, :state] = incoming
+
+            @pl.when(me == j)
+            def _():
+                back[slot] = incoming
+
+            @pl.when(me != j)
+            def _():
+                home(slot, k, j).start()
+
+            incoming = factors[j] * incoming + here
+        return carry
+
+    lax.fori_loop(0, per, link, 0)
+
+    def finish(turn, carry):
+        k = turn // groups
+        owner = (me + turn % groups) % groups
+        chunk = owner * per + k
+
+        @pl.when(owner != me)
+        def _():
+            home_in(chunk).wait_recv()
+
+        carried = mm(readout[...], right_side(back[chunk]))
+        growth = mm(grow[...], expander(chunk, 2 * LANES, hpc, head_dim))
+        obuf[chunk] = obuf[chunk] + carried * growth
+        o_copy(chunk).start()
+        return carry
+
+    lax.fori_loop(0, chunks, finish, 0)
+
+    def drain(chunk, carry):
+        o_copy(chunk).wait()
+
+        @pl.when(chunk // per != me)
+        def _():
+            forth_in(chunk).wait_send()
+            home_in(chunk).wait_send()
+
+        return carry
+
+    lax.fori_loop(0, chunks, drain, 0)
+
+    @pl.when(seq < shards - 1)
+    def _():
+        def drain_chain(k, carry):
+            chain(k).wait_send()
+            return carry
+
+        lax.fori_loop(0, per, drain_chain, 0)
+
+
+def in_one(groups, shards, inputs, log_decay, input_map, output_map, skip_gain):
+    tokens, width = inputs.shape
+    state = input_map.shape[1]
+    chunks = width // CHUNK
+    per = chunks // groups
+    head_dim = width // skip_gain.shape[0]
+    vmem = pl.BlockSpec(memory_space=pltpu.VMEM)
+    anywhere = pl.BlockSpec(memory_space=pl.ANY)
+    f32, bf16 = jnp.float32, jnp.bfloat16
+    dma = pltpu.SemaphoreType.DMA
+    return pl.pallas_call(
+        functools.partial(whole_kernel, groups, shards, head_dim),
+        out_shape=jax.ShapeDtypeStruct((tokens, width), f32),
+        in_specs=[anywhere, vmem, vmem, vmem, vmem],
+        out_specs=anywhere,
+        scratch_shapes=[
+            pltpu.VMEM((chunks, tokens, CHUNK), f32),
+            pltpu.VMEM((chunks, tokens, CHUNK), f32),
+            pltpu.VMEM((chunks, state + 8, CHUNK), f32),
+            pltpu.VMEM((chunks, state + 8, CHUNK), f32),
+            pltpu.VMEM((per, state, CHUNK), f32),
+            pltpu.VMEM((per, state, CHUNK), f32),
+            pltpu.VMEM((chunks, state, CHUNK), f32),
+            pltpu.VMEM((2 * BLOCK + state, 3 * BLOCK), bf16),
+            pltpu.VMEM((BLOCK + state, 3 * BLOCK), bf16),
+            pltpu.VMEM((tokens, 3 * state), bf16),
+            pltpu.VMEM((5 * BLOCK, 2 * LANES), bf16),
+            pltpu.VMEM((2 * BLOCK, 2 * LANES), bf16),
+            pltpu.VMEM((16, 3 * LANES), bf16),
+            dma((chunks,)),
+            dma((chunks,)),
+            dma((chunks,)),
+            dma((chunks,)),
+            dma((per,)),
+            dma((per,)),
+            dma((chunks,)),
+            dma((chunks,)),
+        ],
+        compiler_params=pltpu.CompilerParams(
+            collective_id=0, has_side_effects=True, vmem_limit_bytes=56 << 20
+        ),
+    )(inputs, log_decay, input_map, output_map, skip_gain.reshape(1, -1))
+
+
+def on_any(groups, shards, inputs, log_decay, input_map, output_map, skip_gain):
+    tokens, width = inputs.shape
+    heads = skip_gain.shape[0]
+    head_dim = width // heads
+    fits = (
+        tokens == 2 * BLOCK
+        and input_map.shape[1] == LANES
+        and heads <= LANES
+        and CHUNK % head_dim == 0
+        and width % (groups * CHUNK) == 0
+        and groups > 1
+        and shards > 2
+    )
+    if fits:
+        return in_one(groups, shards, inputs, log_decay, input_map, output_map, skip_gain)
+    return on_device(inputs, log_decay, input_map, output_map, skip_gain)
+
+
 def solution(mesh):
     in_specs = (
         P(("seq", "head"), None),
@@ -131,5 +493,6 @@
     )
     out_specs = P(("seq", "head"), None)
     return jax.shard_map(
-        on_device, mesh=mesh, in_specs=in_specs, out_specs=out_specs, check_vma=False
-    )
+        functools.partial(on_any, mesh.shape["head"], mesh.shape["seq"]),
+        mesh=mesh, in_specs=in_specs, out_specs=out_specs, check_vma=False,
+    )

time: 321 us -> 75.4 us (0.23)
  the two profiles are of different devices: /device:TPU:26 before, /device:TPU:0 now
where the time goes in v1:
time: 75.4 us; the launch traced here: 75.2 us
  Pallas kernels  68.1 us (90%)
  local copies, waits for them, and re-layouts  7.05 us (9%)
    pallas_call x1, Pallas kernels, in_one(): pl.pallas_call(functools.partial(whole_kernel, groups, shards, head_dim),...  68.1 us
    unnamed x2, local copies, waits for them, and re-layouts  7.05 us

profile of v1, /device:TPU:0, one launch (start us, length us, event | category | flops | bytes accessed | tf_op | source)
XLA Modules:
  0.0 75.2 jit_solution(10737694463816067254)
XLA Ops:
  0.0 1.6 %copy.6.d_ref = f32[256,80]{1,0:T(8,128)} copy(f32[256,80]{0,1:T(8,128)} %param.6) | data formatting | bytes 163840 | tf_op args[1]
  1.6 68.1 %shard_map.55 = f32[256,5120]{1,0:T(8,128)} custom-call(f32[256,5120]{1,0:T(8,128)} %x_hbm.1, f32[256,80]{1,0:T(8,128)} %copy.6.d_ref, f32[256,128]{1,0:T(8,128)} %b_ref.1, f32[256,128]{1,0:T(8,128)} %c_ref.1, f32[1,80]{1,0:T(1,128)} %bitcast.1), custom_call_target="tpu_custom_call" | custom-call | tf_op jit(solution)/shard_map/pallas_call | solution.py:434
  69.8 5.4 %copy.8 = f32[256,5120]{1,0:T(8,128)} copy(f32[256,5120]{1,0:T(8,128)} %shard_map.55) | data formatting | bytes 10485760

commit v2 on v1

--- a/solution.py
+++ b/solution.py
@@ -170,10 +170,10 @@
 
 def whole_kernel(
     groups, shards, head_dim,
-    x_hbm, d_ref, b_ref, c_ref, g_ref, o_hbm,
-    xbuf, obuf, mbuf, rbuf, sbuf, sout, back,
-    first, second, readout, spread, grow, rows,
-    xsem, osem, fsend, frecv, csend, crecv, bsend, brecv,
+    x_hbm, d_ref, b_ref, c_ref, g_ref, o_ref,
+    xbuf, mbuf, rbuf, sbuf, sout, back,
+    first, second, readout, spread, grow, rows, loss,
+    xsem, fsend, frecv, csend, crecv, bsend, brecv, lsend, lrecv,
 ):
     seq = lax.axis_index("seq")
     me = lax.axis_index("head")
@@ -186,9 +186,28 @@
         columns = pl.ds(pl.multiple_of(chunk * CHUNK, CHUNK), CHUNK)
         return pltpu.make_async_copy(x_hbm.at[:, columns], xbuf.at[chunk], xsem.at[chunk])
 
-    def o_copy(chunk):
-        columns = pl.ds(pl.multiple_of(chunk * CHUNK, CHUNK), CHUNK)
-        return pltpu.make_async_copy(obuf.at[chunk], o_hbm.at[:, columns], osem.at[chunk])
+    def columns_of(chunk):
+        return pl.ds(pl.multiple_of(chunk * CHUNK, CHUNK), CHUNK)
+
+    def share(step):
+        return pltpu.make_async_remote_copy(
+            src_ref=loss.at[me],
+            dst_ref=loss.at[me],
+            send_sem=lsend.at[step],
+            recv_sem=lrecv.at[me],
+            device_id={"head": (me + step) % groups},
+            device_id_type=MESH,
+        )
+
+    def share_in(source):
+        return pltpu.make_async_remote_copy(
+            src_ref=loss.at[source],
+            dst_ref=loss.at[source],
+            send_sem=lsend.at[0],
+            recv_sem=lrecv.at[source],
+            device_id={"head": (me + 1) % groups},
+            device_id_type=MESH,
+        )
 
     def at_turn(turn):
         k = turn // groups
@@ -227,7 +246,7 @@
 
     def home(slot, k, target):
         return pltpu.make_async_remote_copy(
-            src_ref=rbuf.at[slot, pl.ds(0, state)],
+            src_ref=rbuf.at[slot],
             dst_ref=back.at[me * per + k],
             send_sem=bsend.at[slot],
             recv_sem=brecv.at[me * per + k],
@@ -237,7 +256,7 @@
 
     def home_in(slot):
         return pltpu.make_async_remote_copy(
-            src_ref=rbuf.at[slot, pl.ds(0, state)],
+            src_ref=rbuf.at[slot],
             dst_ref=back.at[slot],
             send_sem=bsend.at[slot],
             recv_sem=brecv.at[slot],
@@ -261,13 +280,13 @@
             barrier, inc=1, device_id={"seq": (seq + step) % shards}, device_id_type=MESH
         )
 
-    heads = d_ref.shape[1]
+    heads = d_ref.shape[0]
     below = lax.broadcasted_iota(jnp.int32, (BLOCK, BLOCK), 0)
     above = lax.broadcasted_iota(jnp.int32, (BLOCK, BLOCK), 1)
     causal = below >= above
     ones = jnp.where(causal, 1.0, 0.0).astype(jnp.bfloat16)
-    padding = jnp.zeros((d_ref.shape[0], LANES - heads), jnp.float32)
-    decay = jnp.concatenate([d_ref[...], padding], axis=1)
+    padding = jnp.zeros((LANES - heads, d_ref.shape[1]), jnp.float32)
+    decay = jnp.concatenate([d_ref[...], padding], axis=0).T
     run1 = sum(mm(ones, part) for part in three(decay[:BLOCK]))
     run2 = sum(mm(ones, part) for part in three(decay[BLOCK:]))
     end1, end2 = run1[BLOCK - 1 :], run2[BLOCK - 1 :]
@@ -289,11 +308,11 @@
     )
     gain = jnp.concatenate([g_ref[...], jnp.zeros((1, LANES - heads), jnp.float32)], axis=1)
     line = lax.broadcasted_iota(jnp.int32, (16, LANES), 0)
-    picked = jnp.where(line == 0, jnp.exp(total), 0.0)
-    picked = jnp.where(line == 1, jnp.exp(total - mid1), picked)
+    picked = jnp.where(line == 1, jnp.exp(total - mid1), 0.0)
     picked = jnp.where(line == 2, jnp.exp(end2 - mid2), picked)
     picked = jnp.where(line == 3, gain, picked)
     rows[...] = jnp.concatenate(three(picked), axis=1)
+    loss[me] = jnp.broadcast_to(jnp.exp(total), (8, LANES))
 
     b1, b2 = b_ref[:BLOCK], b_ref[BLOCK:]
     c1, c2 = c_ref[:BLOCK], c_ref[BLOCK:]
@@ -310,6 +329,8 @@
         sbuf[...] = jnp.zeros_like(sbuf)
 
     pl.semaphore_wait(barrier, groups + 1)
+    for step in range(1, groups):
+        share(step).start()
 
     def local(turn, carry):
         k, owner, chunk = at_turn(turn)
@@ -320,38 +341,45 @@
         weighed = x * scale[: 2 * BLOCK]
         y1 = mm(first[...], right_side(weighed[:BLOCK]))
         y2 = mm(second[...], right_side(weighed[BLOCK:]))
-        obuf[chunk, :BLOCK] = y1[:BLOCK] * scale[2 * BLOCK : 3 * BLOCK] + lines[3:4] * x[:BLOCK]
-        obuf[chunk, BLOCK:] = (
+        o_ref[:BLOCK, columns_of(chunk)] = y1[:BLOCK] * scale[2 * BLOCK : 3 * BLOCK] + lines[3:4] * x[:BLOCK]
+        o_ref[BLOCK:, columns_of(chunk)] = (
             y2[:BLOCK] * scale[3 * BLOCK : 4 * BLOCK]
             + y1[BLOCK : 2 * BLOCK] * scale[4 * BLOCK :]
             + lines[3:4] * x[BLOCK:]
         )
         memory = y1[2 * BLOCK :] * lines[1:2] + y2[BLOCK:] * lines[2:3]
-        factor = jnp.broadcast_to(lines[0:1], (8, CHUNK))
 
         @pl.when(owner == me)
         def _():
-            rbuf[chunk, :state] = memory
-            rbuf[chunk, state:] = factor
+            rbuf[chunk] = memory
 
         @pl.when(owner != me)
         def _():
-            mbuf[chunk, :state] = memory
-            mbuf[chunk, state:] = factor
+            mbuf[chunk] = memory
             forth(chunk, k, owner).start()
 
         return carry
 
     lax.fori_loop(0, chunks, local, 0)
+
+    for step in range(1, groups):
+        share_in((me + step) % groups).wait_recv()
+    tall = -(-groups // 16) * 16
+    line = lax.broadcasted_iota(jnp.int32, (tall, LANES), 0)
+    losses = jnp.zeros((tall, LANES), jnp.float32)
+    for j in range(groups):
+        losses = jnp.where(line == j, loss[j, :1], losses)
+    losses = jnp.concatenate(three(losses), axis=1)
 
     def link(k, carry):
         for step in range(1, groups):
             forth_in(((me + step) % groups) * per + k).wait_recv()
-        factors = [rbuf[j * per + k, state : state + 1] for j in range(groups)]
-        shard = rbuf[k, :state]
+        wide = mm(losses, expander(me * per + k, 3 * LANES, hpc, head_dim))
+        factors = [wide[j : j + 1] for j in range(groups)]
+        shard = rbuf[k]
         shard_factor = factors[0]
         for j in range(1, groups):
-            shard = factors[j] * shard + rbuf[j * per + k, :state]
+            shard = factors[j] * shard + rbuf[j * per + k]
             shard_factor = shard_factor * factors[j]
         sout[k] = shard
 
@@ -367,8 +395,8 @@
         incoming = sbuf[k]
         for j in range(groups):
             slot = j * per + k
-            here = rbuf[slot, :state]
-            rbuf[slot, :state] = incoming
+            here = rbuf[slot]
+            rbuf[slot] = incoming
 
             @pl.when(me == j)
             def _():
@@ -394,15 +422,13 @@
 
         carried = mm(readout[...], right_side(back[chunk]))
         growth = mm(grow[...], expander(chunk, 2 * LANES, hpc, head_dim))
-        obuf[chunk] = obuf[chunk] + carried * growth
-        o_copy(chunk).start()
+        columns = columns_of(chunk)
+        o_ref[:, columns] = o_ref[:, columns] + carried * growth
         return carry
 
     lax.fori_loop(0, chunks, finish, 0)
 
     def drain(chunk, carry):
-        o_copy(chunk).wait()
-
         @pl.when(chunk // per != me)
         def _():
             forth_in(chunk).wait_send()
@@ -411,6 +437,8 @@
         return carry
 
     lax.fori_loop(0, chunks, drain, 0)
+    for step in range(1, groups):
+        share(step).wait_send()
 
     @pl.when(seq < shards - 1)
     def _():
@@ -428,19 +456,18 @@
     per = chunks // groups
     head_dim = width // skip_gain.shape[0]
     vmem = pl.BlockSpec(memory_space=pltpu.VMEM)
-    anywhere = pl.BlockSpec(memory_space=pl.ANY)
+    far = pl.BlockSpec(memory_space=pltpu.HBM)
     f32, bf16 = jnp.float32, jnp.bfloat16
     dma = pltpu.SemaphoreType.DMA
     return pl.pallas_call(
         functools.partial(whole_kernel, groups, shards, head_dim),
         out_shape=jax.ShapeDtypeStruct((tokens, width), f32),
-        in_specs=[anywhere, vmem, vmem, vmem, vmem],
-        out_specs=anywhere,
+        in_specs=[far, vmem, vmem, vmem, vmem],
+        out_specs=vmem,
         scratch_shapes=[
             pltpu.VMEM((chunks, tokens, CHUNK), f32),
-            pltpu.VMEM((chunks, tokens, CHUNK), f32),
-            pltpu.VMEM((chunks, state + 8, CHUNK), f32),
-            pltpu.VMEM((chunks, state + 8, CHUNK), f32),
+            pltpu.VMEM((chunks, state, CHUNK), f32),
+            pltpu.VMEM((chunks, state, CHUNK), f32),
             pltpu.VMEM((per, state, CHUNK), f32),
             pltpu.VMEM((per, state, CHUNK), f32),
             pltpu.VMEM((chunks, state, CHUNK), f32),
@@ -450,7 +477,7 @@
             pltpu.VMEM((5 * BLOCK, 2 * LANES), bf16),
             pltpu.VMEM((2 * BLOCK, 2 * LANES), bf16),
             pltpu.VMEM((16, 3 * LANES), bf16),
-            dma((chunks,)),
+            pltpu.VMEM((groups, 8, LANES), f32),
             dma((chunks,)),
             dma((chunks,)),
             dma((chunks,)),
@@ -458,11 +485,13 @@
             dma((per,)),
             dma((chunks,)),
             dma((chunks,)),
+            dma((groups,)),
+            dma((groups,)),
         ],
         compiler_params=pltpu.CompilerParams(
-            collective_id=0, has_side_effects=True, vmem_limit_bytes=56 << 20
+            collective_id=0, has_side_effects=True, vmem_limit_bytes=36 << 20
         ),
-    )(inputs, log_decay, input_map, output_map, skip_gain.reshape(1, -1))
+    )(inputs, log_decay.T, input_map, output_map, skip_gain.reshape(1, -1))
 
 
 def on_any(groups, shards, inputs, log_decay, input_map, output_map, skip_gain):

time: 75.4 us -> 74.1 us (0.983)
  Pallas kernels: 68.1 us -> 65.6 us
  local copies, waits for them, and re-layouts: 7.05 us -> 8.19 us
    pallas_call x1, Pallas kernels: 68.1 us -> 65.6 us  [in_one(): pl.pallas_call(functools.partial(whole_kernel, groups, shards, head_dim),...]
    unnamed x2 -> x11, local copies, waits for them, and re-layouts: 7.05 us -> 8.19 us
where the time goes in v2:
time: 74.1 us; the launch traced here: 73.8 us
  Pallas kernels  65.6 us (89%)
  local copies, waits for them, and re-layouts  8.19 us (11%)
    pallas_call x1, Pallas kernels, in_one(): pl.pallas_call(functools.partial(whole_kernel, groups, shards, head_dim),...  65.6 us
    unnamed x11, local copies, waits for them, and re-layouts  8.19 us

profile of v2, /device:TPU:0, one launch (start us, length us, event | category | flops | bytes accessed | tf_op | source)
XLA Modules:
  0.0 73.8 jit_solution(17101482288992743359)
XLA Ops:
  0.0 0.0 copy-start
  0.0 2.5 %copy-done = f32[256,5120]{1,0:T(8,128)S(1)} copy-done((f32[256,5120]{1,0:T(8,128)S(1)}, f32[256,5120]{1,0:T(8,128)}, u32[]{:S(2)}) %copy-start) | copy-done | bytes 5242904
  2.5 0.0 copy-start.1
  2.5 0.9 %copy-done.1 = f32[256,128]{1,0:T(8,128)S(1)} copy-done((f32[256,128]{1,0:T(8,128)S(1)}, f32[256,128]{1,0:T(8,128)}, u32[]{:S(2)}) %copy-start.1) | copy-done | bytes 131096
  3.4 0.0 copy-start.2
  3.4 0.9 %copy-done.2 = f32[256,128]{1,0:T(8,128)S(1)} copy-done((f32[256,128]{1,0:T(8,128)S(1)}, f32[256,128]{1,0:T(8,128)}, u32[]{:S(2)}) %copy-start.2) | copy-done | bytes 131096
  4.3 0.0 copy-start.3
  4.3 0.9 %copy-done.3 = f32[256,80]{0,1:T(8,128)S(1)} copy-done((f32[256,80]{0,1:T(8,128)S(1)}, f32[256,80]{0,1:T(8,128)}, u32[]{:S(2)}) %copy-start.3) | copy-done | bytes 81944
  5.2 0.0 copy-start.4
  5.2 0.7 copy-done.4
  5.8 65.6 %shard_map.55 = f32[256,5120]{1,0:T(8,128)S(1)} custom-call(f32[256,5120]{1,0:T(8,128)S(1)} %copy-done, f32[80,256]{1,0:T(8,128)S(1)} %bitcast.2, f32[256,128]{1,0:T(8,128)S(1)} %copy-done.1, f32[256,128]{1,0:T(8,128)S(1)} %copy-done.2, f32[1,80]{1,0:T(1,128)S(1)} %bitcast.3), custom_call_target="tpu_custom_call" | custom-call | tf_op jit(solution)/shard_map/pallas_call | solution.py:462
  71.5 2.4 %copy.7 = f32[256,5120]{1,0:T(8,128)} copy(f32[256,5120]{1,0:T(8,128)S(1)} %shard_map.55) | data formatting | bytes 10485760
Async XLA Ops:
  0.0 2.5 %copy-start = (f32[256,5120]{1,0:T(8,128)S(1)}, f32[256,5120]{1,0:T(8,128)}, u32[]{:S(2)}) copy-start(f32[256,5120]{1,0:T(8,128)} %x_hbm.1) | copy-start | bytes 15728644
  2.5 0.9 %copy-start.1 = (f32[256,128]{1,0:T(8,128)S(1)}, f32[256,128]{1,0:T(8,128)}, u32[]{:S(2)}) copy-start(f32[256,128]{1,0:T(8,128)} %b_ref.1) | copy-start | bytes 393220
  3.4 0.9 %copy-start.2 = (f32[256,128]{1,0:T(8,128)S(1)}, f32[256,128]{1,0:T(8,128)}, u32[]{:S(2)}) copy-start(f32[256,128]{1,0:T(8,128)} %c_ref.1) | copy-start | bytes 393220
  4.3 0.9 %copy-start.3 = (f32[256,80]{0,1:T(8,128)S(1)}, f32[256,80]{0,1:T(8,128)}, u32[]{:S(2)}) copy-start(f32[256,80]{0,1:T(8,128)} %param.6) | copy-start | bytes 245764
  5.2 0.7 copy-start.4

commit v3 on v2

--- a/solution.py
+++ b/solution.py
@@ -491,7 +491,12 @@
         compiler_params=pltpu.CompilerParams(
             collective_id=0, has_side_effects=True, vmem_limit_bytes=36 << 20
         ),
-    )(inputs, log_decay.T, input_map, output_map, skip_gain.reshape(1, -1))
+    )(
+        *(
+            pltpu.with_memory_space_constraint(operand, pltpu.HBM)
+            for operand in (inputs, log_decay.T, input_map, output_map, skip_gain.reshape(1, -1))
+        )
+    )
 
 
 def on_any(groups, shards, inputs, log_decay, input_map, output_map, skip_gain):

time: 74.1 us -> 68.5 us (0.924)
  local copies, waits for them, and re-layouts: 8.19 us -> 2.36 us
    unnamed x11 -> x1, local copies, waits for them, and re-layouts: 8.19 us -> 2.36 us
where the time goes in v3:
time: 68.5 us; the launch traced here: 68.4 us
  Pallas kernels  66 us (96%)
  local copies, waits for them, and re-layouts  2.36 us (3%)
    pallas_call x1, Pallas kernels, in_one(): pl.pallas_call(functools.partial(whole_kernel, groups, shards, head_dim),...  66 us
    unnamed x1, local copies, waits for them, and re-layouts  2.36 us

profile of v3, /device:TPU:0, one launch (start us, length us, event | category | flops | bytes accessed | tf_op | source)
XLA Modules:
  0.0 68.4 jit_solution(6449336246877197084)
XLA Ops:
  0.0 66.0 %shard_map.55 = f32[256,5120]{1,0:T(8,128)S(1)} custom-call(f32[256,5120]{1,0:T(8,128)} %x_hbm.1, f32[80,256]{1,0:T(8,128)} %bitcast.2, f32[256,128]{1,0:T(8,128)} %b_ref.1, f32[256,128]{1,0:T(8,128)} %c_ref.1, f32[1,80]{1,0:T(1,128)} %bitcast.3), custom_call_target="tpu_custom_call" | custom-call | tf_op jit(solution)/shard_map/pallas_call | solution.py:462
  66.0 2.4 %copy.7 = f32[256,5120]{1,0:T(8,128)} copy(f32[256,5120]{1,0:T(8,128)S(1)} %shard_map.55) | data formatting | bytes 10485760

commit v4 on v3

--- a/solution.py
+++ b/solution.py
@@ -170,10 +170,10 @@
 
 def whole_kernel(
     groups, shards, head_dim,
-    x_hbm, d_ref, b_ref, c_ref, g_ref, o_ref,
-    xbuf, mbuf, rbuf, sbuf, sout, back,
-    first, second, readout, spread, grow, rows, loss,
-    xsem, fsend, frecv, csend, crecv, bsend, brecv, lsend, lrecv,
+    x_hbm, d_hbm, b_hbm, c_hbm, g_hbm, o_ref,
+    d_ref, b_ref, c_ref, g_ref, xbuf, mbuf, rbuf, sbuf, sout, back,
+    state1, state2, first, second, readout, lift, spread, grow, rows, loss,
+    isem, xsem, fsend, frecv, csend, crecv, bsend, brecv, lsend, lrecv,
 ):
     seq = lax.axis_index("seq")
     me = lax.axis_index("head")
@@ -268,8 +268,6 @@
         x_copy(at_turn(turn)[2]).start()
         return carry
 
-    lax.fori_loop(0, chunks, load, 0)
-
     barrier = pltpu.get_barrier_semaphore()
     for step in range(1, groups):
         pl.semaphore_signal(
@@ -279,12 +277,21 @@
         pl.semaphore_signal(
             barrier, inc=1, device_id={"seq": (seq + step) % shards}, device_id_type=MESH
         )
+
+    pairs = ((d_hbm, d_ref), (b_hbm, b_ref), (g_hbm, g_ref), (c_hbm, c_ref))
+    small = [pltpu.make_async_copy(*pair, isem.at[i]) for i, pair in enumerate(pairs)]
+    small[0].start()
+    small[1].start()
+    small[2].start()
+    lax.fori_loop(0, chunks, load, 0)
+    small[3].start()
 
     heads = d_ref.shape[0]
     below = lax.broadcasted_iota(jnp.int32, (BLOCK, BLOCK), 0)
     above = lax.broadcasted_iota(jnp.int32, (BLOCK, BLOCK), 1)
     causal = below >= above
     ones = jnp.where(causal, 1.0, 0.0).astype(jnp.bfloat16)
+    small[0].wait()
     padding = jnp.zeros((LANES - heads, d_ref.shape[1]), jnp.float32)
     decay = jnp.concatenate([d_ref[...], padding], axis=0).T
     run1 = sum(mm(ones, part) for part in three(decay[:BLOCK]))
@@ -292,20 +299,9 @@
     end1, end2 = run1[BLOCK - 1 :], run2[BLOCK - 1 :]
     mid1, mid2 = run1[BLOCK // 2 - 1 : BLOCK // 2], run2[BLOCK // 2 - 1 : BLOCK // 2]
     total = end1 + end2
-    tables = jnp.concatenate(
-        [
-            jnp.exp(mid1 - run1),
-            jnp.exp(mid2 - run2),
-            jnp.exp(run1 - mid1),
-            jnp.exp(run2 - mid2),
-            jnp.exp(run2 + (end1 - mid1)),
-        ],
-        axis=0,
-    )
-    spread[...] = jnp.concatenate(two(tables), axis=1)
-    grow[...] = jnp.concatenate(
-        two(jnp.concatenate([jnp.exp(run1), jnp.exp(run2 + end1)], axis=0)), axis=1
-    )
+    up = jnp.concatenate([jnp.exp(mid1 - run1), jnp.exp(mid2 - run2)], axis=0)
+    lift[...] = jnp.concatenate(two(up), axis=1)
+    small[2].wait()
     gain = jnp.concatenate([g_ref[...], jnp.zeros((1, LANES - heads), jnp.float32)], axis=1)
     line = lax.broadcasted_iota(jnp.int32, (16, LANES), 0)
     picked = jnp.where(line == 1, jnp.exp(total - mid1), 0.0)
@@ -313,55 +309,83 @@
     picked = jnp.where(line == 3, gain, picked)
     rows[...] = jnp.concatenate(three(picked), axis=1)
     loss[me] = jnp.broadcast_to(jnp.exp(total), (8, LANES))
-
+    small[1].wait()
     b1, b2 = b_ref[:BLOCK], b_ref[BLOCK:]
+    state1[...] = left_side(b1.T)
+    state2[...] = left_side(b2.T)
+
+    @pl.when(seq == 0)
+    def _():
+        sbuf[...] = jnp.zeros_like(sbuf)
+
+    pl.semaphore_wait(barrier, groups + 1)
+    for step in range(1, groups):
+        share(step).start()
+
+    def weighed(chunk):
+        scale = mm(lift[...], expander(chunk, 2 * LANES, hpc, head_dim))
+        value = xbuf[chunk] * scale
+        return right_side(value[:BLOCK]), right_side(value[BLOCK:])
+
+    def send(turn, carry):
+        k, owner, chunk = at_turn(turn)
+        x_copy(chunk).wait()
+        w1, w2 = weighed(chunk)
+        lines = mm(rows[...], expander(chunk, 3 * LANES, hpc, head_dim))
+        memory = mm(state1[...], w1) * lines[1:2] + mm(state2[...], w2) * lines[2:3]
+
+        @pl.when(owner == me)
+        def _():
+            rbuf[chunk] = memory
+
+        @pl.when(owner != me)
+        def _():
+            mbuf[chunk] = memory
+            forth(chunk, k, owner).start()
+
+        return carry
+
+    lax.fori_loop(0, chunks, send, 0)
+
+    down = jnp.concatenate(
+        [
+            jnp.exp(run1 - mid1),
+            jnp.exp(run2 - mid2),
+            jnp.exp(run2 + (end1 - mid1)),
+        ],
+        axis=0,
+    )
+    spread[...] = jnp.concatenate(two(down), axis=1)
+    grow[...] = jnp.concatenate(
+        two(jnp.concatenate([jnp.exp(run1), jnp.exp(run2 + end1)], axis=0)), axis=1
+    )
+    small[3].wait()
     c1, c2 = c_ref[:BLOCK], c_ref[BLOCK:]
     last = ((1,), (1,))
     own1 = jnp.where(causal, full_mm(c1, b1, last), 0.0)
     own2 = jnp.where(causal, full_mm(c2, b2, last), 0.0)
     cross = full_mm(c2, b1, last)
-    first[...] = left_side(jnp.concatenate([own1, cross, b1.T], axis=0))
-    second[...] = left_side(jnp.concatenate([own2, b2.T], axis=0))
+    first[...] = left_side(jnp.concatenate([own1, cross], axis=0))
+    second[...] = left_side(own2)
     readout[...] = left_side(c_ref[...])
-
-    @pl.when(seq == 0)
-    def _():
-        sbuf[...] = jnp.zeros_like(sbuf)
-
-    pl.semaphore_wait(barrier, groups + 1)
-    for step in range(1, groups):
-        share(step).start()
 
     def local(turn, carry):
         k, owner, chunk = at_turn(turn)
-        x_copy(chunk).wait()
-        x = xbuf[chunk]
+        w1, w2 = weighed(chunk)
         scale = mm(spread[...], expander(chunk, 2 * LANES, hpc, head_dim))
         lines = mm(rows[...], expander(chunk, 3 * LANES, hpc, head_dim))
-        weighed = x * scale[: 2 * BLOCK]
-        y1 = mm(first[...], right_side(weighed[:BLOCK]))
-        y2 = mm(second[...], right_side(weighed[BLOCK:]))
-        o_ref[:BLOCK, columns_of(chunk)] = y1[:BLOCK] * scale[2 * BLOCK : 3 * BLOCK] + lines[3:4] * x[:BLOCK]
-        o_ref[BLOCK:, columns_of(chunk)] = (
-            y2[:BLOCK] * scale[3 * BLOCK : 4 * BLOCK]
-            + y1[BLOCK : 2 * BLOCK] * scale[4 * BLOCK :]
-            + lines[3:4] * x[BLOCK:]
-        )
-        memory = y1[2 * BLOCK :] * lines[1:2] + y2[BLOCK:] * lines[2:3]
-
-        @pl.when(owner == me)
-        def _():
-            rbuf[chunk] = memory
-
-        @pl.when(owner != me)
-        def _():
-            mbuf[chunk] = memory
-            forth(chunk, k, owner).start()
-
+        y1 = mm(first[...], w1)
+        y2 = mm(second[...], w2)
+        columns = columns_of(chunk)
+        o_ref[:BLOCK, columns] = y1[:BLOCK] * scale[:BLOCK] + lines[3:4] * xbuf[chunk, :BLOCK]
+        o_ref[BLOCK:, columns] = (
+            y2 * scale[BLOCK : 2 * BLOCK]
+            + y1[BLOCK:] * scale[2 * BLOCK :]
+            + lines[3:4] * xbuf[chunk, BLOCK:]
+        )
         return carry
 
-    lax.fori_loop(0, chunks, local, 0)
-
+    lax.fori_loop(0, groups, local, 0)
     for step in range(1, groups):
         share_in((me + step) % groups).wait_recv()
     tall = -(-groups // 16) * 16
@@ -372,6 +396,9 @@
     losses = jnp.concatenate(three(losses), axis=1)
 
     def link(k, carry):
+        lax.fori_loop(
+            jnp.minimum((k + 1) * groups, chunks), jnp.minimum((k + 2) * groups, chunks), local, 0
+        )
         for step in range(1, groups):
             forth_in(((me + step) % groups) * per + k).wait_recv()
         wide = mm(losses, expander(me * per + k, 3 * LANES, hpc, head_dim))
@@ -462,22 +489,30 @@
     return pl.pallas_call(
         functools.partial(whole_kernel, groups, shards, head_dim),
         out_shape=jax.ShapeDtypeStruct((tokens, width), f32),
-        in_specs=[far, vmem, vmem, vmem, vmem],
+        in_specs=[far] * 5,
         out_specs=vmem,
         scratch_shapes=[
+            pltpu.VMEM(log_decay.shape[::-1], f32),
+            pltpu.VMEM(input_map.shape, f32),
+            pltpu.VMEM(output_map.shape, f32),
+            pltpu.VMEM((1, skip_gain.shape[0]), f32),
             pltpu.VMEM((chunks, tokens, CHUNK), f32),
             pltpu.VMEM((chunks, state, CHUNK), f32),
             pltpu.VMEM((chunks, state, CHUNK), f32),
             pltpu.VMEM((per, state, CHUNK), f32),
             pltpu.VMEM((per, state, CHUNK), f32),
             pltpu.VMEM((chunks, state, CHUNK), f32),
-            pltpu.VMEM((2 * BLOCK + state, 3 * BLOCK), bf16),
-            pltpu.VMEM((BLOCK + state, 3 * BLOCK), bf16),
+            pltpu.VMEM((state, 3 * BLOCK), bf16),
+            pltpu.VMEM((state, 3 * BLOCK), bf16),
+            pltpu.VMEM((2 * BLOCK, 3 * BLOCK), bf16),
+            pltpu.VMEM((BLOCK, 3 * BLOCK), bf16),
             pltpu.VMEM((tokens, 3 * state), bf16),
-            pltpu.VMEM((5 * BLOCK, 2 * LANES), bf16),
+            pltpu.VMEM((2 * BLOCK, 2 * LANES), bf16),
+            pltpu.VMEM((3 * BLOCK, 2 * LANES), bf16),
             pltpu.VMEM((2 * BLOCK, 2 * LANES), bf16),
             pltpu.VMEM((16, 3 * LANES), bf16),
             pltpu.VMEM((groups, 8, LANES), f32),
+            dma((4,)),
             dma((chunks,)),
             dma((chunks,)),
             dma((chunks,)),

time: 68.5 us -> 67.2 us (0.981)
  Pallas kernels: 66 us -> 64.7 us
    pallas_call x1, Pallas kernels: 66 us -> 64.7 us  [in_one(): pl.pallas_call(functools.partial(whole_kernel, groups, shards, head_dim),...]
where the time goes in v4:
time: 67.2 us; the launch traced here: 67.1 us
  Pallas kernels  64.7 us (96%)
  local copies, waits for them, and re-layouts  2.36 us (4%)
    pallas_call x1, Pallas kernels, in_one(): pl.pallas_call(functools.partial(whole_kernel, groups, shards, head_dim),...  64.7 us
    unnamed x1, local copies, waits for them, and re-layouts  2.36 us

profile of v4, /device:TPU:0, one launch (start us, length us, event | category | flops | bytes accessed | tf_op | source)
XLA Modules:
  0.0 67.1 jit_solution(8344735964520820116)
XLA Ops:
  0.0 64.7 %shard_map.55 = f32[256,5120]{1,0:T(8,128)S(1)} custom-call(f32[256,5120]{1,0:T(8,128)} %x_hbm.1, f32[80,256]{1,0:T(8,128)} %bitcast.2, f32[256,128]{1,0:T(8,128)} %b_hbm.1, f32[256,128]{1,0:T(8,128)} %c_hbm.1, f32[1,80]{1,0:T(1,128)} %bitcast.3), custom_call_target="tpu_custom_call" | custom-call | tf_op jit(solution)/shard_map/pallas_call | solution.py:489
  64.7 2.4 %copy.7 = f32[256,5120]{1,0:T(8,128)} copy(f32[256,5120]{1,0:T(8,128)S(1)} %shard_map.55) | data formatting | bytes 10485760

commit v5 on v4

--- a/solution.py
+++ b/solution.py
@@ -170,9 +170,9 @@
 
 def whole_kernel(
     groups, shards, head_dim,
-    x_hbm, d_hbm, b_hbm, c_hbm, g_hbm, o_ref,
+    x_hbm, d_hbm, b_hbm, c_hbm, g_hbm, o_ref, late, grow, readout,
     d_ref, b_ref, c_ref, g_ref, xbuf, mbuf, rbuf, sbuf, sout, back,
-    state1, state2, first, second, readout, lift, spread, grow, rows, loss,
+    state1, state2, first, second, lift, spread, rows, loss,
     isem, xsem, fsend, frecv, csend, crecv, bsend, brecv, lsend, lrecv,
 ):
     seq = lax.axis_index("seq")
@@ -453,7 +453,20 @@
         o_ref[:, columns] = o_ref[:, columns] + carried * growth
         return carry
 
-    lax.fori_loop(0, chunks, finish, 0)
+    lax.fori_loop(0, chunks - groups, finish, 0)
+
+    def arrive(turn, carry):
+        owner = (me + turn) % groups
+        chunk = owner * per + per - 1
+
+        @pl.when(owner != me)
+        def _():
+            home_in(chunk).wait_recv()
+
+        late[owner] = back[chunk]
+        return carry
+
+    lax.fori_loop(0, groups, arrive, 0)
 
     def drain(chunk, carry):
         @pl.when(chunk // per != me)
@@ -474,6 +487,31 @@
             return carry
 
         lax.fori_loop(0, per, drain_chain, 0)
+
+
+def closing_kernel(groups, head_dim, part, late, grow, readout, o_hbm, ready, sem):
+    chunks = part.shape[1] // CHUNK
+    per = chunks // groups
+    copies = []
+    for chunk in range(chunks):
+        columns = pl.ds(chunk * CHUNK, CHUNK)
+        if chunk % per < per - 1:
+            copies.append(
+                pltpu.make_async_copy(part.at[:, columns], o_hbm.at[:, columns], sem.at[chunk])
+            )
+            copies[-1].start()
+    for owner in range(groups):
+        chunk = owner * per + per - 1
+        columns = pl.ds(chunk * CHUNK, CHUNK)
+        carried = mm(readout[...], right_side(late[owner]))
+        growth = mm(grow[...], expander(chunk, 2 * LANES, CHUNK // head_dim, head_dim))
+        ready[owner] = part[:, columns] + carried * growth
+        copies.append(
+            pltpu.make_async_copy(ready.at[owner], o_hbm.at[:, columns], sem.at[chunk])
+        )
+        copies[-1].start()
+    for copy in copies:
+        copy.wait()
 
 
 def in_one(groups, shards, inputs, log_decay, input_map, output_map, skip_gain):
@@ -486,11 +524,16 @@
     far = pl.BlockSpec(memory_space=pltpu.HBM)
     f32, bf16 = jnp.float32, jnp.bfloat16
     dma = pltpu.SemaphoreType.DMA
-    return pl.pallas_call(
+    parts = pl.pallas_call(
         functools.partial(whole_kernel, groups, shards, head_dim),
-        out_shape=jax.ShapeDtypeStruct((tokens, width), f32),
+        out_shape=(
+            jax.ShapeDtypeStruct((tokens, width), f32),
+            jax.ShapeDtypeStruct((groups, state, CHUNK), f32),
+            jax.ShapeDtypeStruct((tokens, 2 * LANES), bf16),
+            jax.ShapeDtypeStruct((tokens, 3 * state), bf16),
+        ),
         in_specs=[far] * 5,
-        out_specs=vmem,
+        out_specs=[vmem] * 4,
         scratch_shapes=[
             pltpu.VMEM(log_decay.shape[::-1], f32),
             pltpu.VMEM(input_map.shape, f32),
@@ -506,10 +549,8 @@
             pltpu.VMEM((state, 3 * BLOCK), bf16),
             pltpu.VMEM((2 * BLOCK, 3 * BLOCK), bf16),
             pltpu.VMEM((BLOCK, 3 * BLOCK), bf16),
-            pltpu.VMEM((tokens, 3 * state), bf16),
             pltpu.VMEM((2 * BLOCK, 2 * LANES), bf16),
             pltpu.VMEM((3 * BLOCK, 2 * LANES), bf16),
-            pltpu.VMEM((2 * BLOCK, 2 * LANES), bf16),
             pltpu.VMEM((16, 3 * LANES), bf16),
             pltpu.VMEM((groups, 8, LANES), f32),
             dma((4,)),
@@ -532,6 +573,14 @@
             for operand in (inputs, log_decay.T, input_map, output_map, skip_gain.reshape(1, -1))
         )
     )
+    return pl.pallas_call(
+        functools.partial(closing_kernel, groups, head_dim),
+        out_shape=jax.ShapeDtypeStruct((tokens, width), f32),
+        in_specs=[vmem] * 4,
+        out_specs=pl.BlockSpec(memory_space=pl.ANY),
+        scratch_shapes=[pltpu.VMEM((groups, tokens, CHUNK), f32), dma((chunks,))],
+        compiler_params=pltpu.CompilerParams(vmem_limit_bytes=16 << 20),
+    )(*parts)
 
 
 def on_any(groups, shards, inputs, log_decay, input_map, output_map, skip_gain):

time: 67.2 us -> 66.9 us (level)
  local copies, waits for them, and re-layouts: 2.36 us -> 0 us
  Pallas kernels: 64.7 us -> 66.7 us
    pallas_call x0 -> x1, Pallas kernels: none -> 2.5 us  [in_one(): pl.pallas_call(functools.partial(closing_kernel, groups, head_dim), out_s...]
    unnamed x1 -> x0, local copies, waits for them, and re-layouts: 2.36 us -> none
where the time goes in v5:
time: 66.9 us; the launch traced here: 66.7 us
  Pallas kernels  66.7 us (100%)
    pallas_call x1, Pallas kernels, in_one(): pl.pallas_call(functools.partial(whole_kernel, groups, shards, head_dim),...  64.2 us
    pallas_call x1, Pallas kernels, in_one(): pl.pallas_call(functools.partial(closing_kernel, groups, head_dim), out_s...  2.5 us

profile of v5, /device:TPU:0, one launch (start us, length us, event | category | flops | bytes accessed | tf_op | source)
XLA Modules:
  0.0 66.7 jit_solution(15351236725008854138)
XLA Ops:
  0.0 64.2 %shard_map.55 = (f32[256,5120]{1,0:T(8,128)S(1)}, f32[4,128,256]{2,1,0:T(8,128)S(1)}, bf16[256,256]{1,0:T(8,128)(2,1)S(1)}, bf16[256,384]{1,0:T(8,128)(2,1)S(1)}) custom-call(f32[256,5120]{1,0:T(8,128)} %x_hbm.1, f32[80,256]{1,0:T(8,128)} %bitcast.2, f32[256,128]{1,0:T(8,128)} %b_hbm.1, f32[256,128]{1,0:T(8,128)} %c_hbm.1, f32[1,80]{1,0:T(1,128)} %bitcast.3), custom_call_target="tpu_custom_call" | custom-call | tf_op jit(solution)/shard_map/pallas_call | solution.py:527
  64.2 2.5 %shard_map.56 = f32[256,5120]{1,0:T(8,128)} custom-call(f32[256,5120]{1,0:T(8,128)S(1)} %get-tuple-element.9.part, f32[4,128,256]{2,1,0:T(8,128)S(1)} %get-tuple-element.10.late, bf16[256,256]{1,0:T(8,128)(2,1)S(1)} %get-tuple-element.11.grow, bf16[256,384]{1,0:T(8,128)(2,1)S(1)} %get-tuple-element.12.readout), custom_call_target="tpu_custom_call" | custom-call | tf_op jit(solution)/shard_map/pallas_call | solution.py:576

commit v6 on v5

--- a/solution.py
+++ b/solution.py
@@ -273,9 +273,11 @@
         pl.semaphore_signal(
             barrier, inc=1, device_id={"head": (me + step) % groups}, device_id_type=MESH
         )
-    for step in (1, shards - 1):
+
+    @pl.when(seq > 0)
+    def _():
         pl.semaphore_signal(
-            barrier, inc=1, device_id={"seq": (seq + step) % shards}, device_id_type=MESH
+            barrier, inc=1, device_id={"seq": (seq + shards - 1) % shards}, device_id_type=MESH
         )
 
     pairs = ((d_hbm, d_ref), (b_hbm, b_ref), (g_hbm, g_ref), (c_hbm, c_ref))
@@ -318,7 +320,7 @@
     def _():
         sbuf[...] = jnp.zeros_like(sbuf)
 
-    pl.semaphore_wait(barrier, groups + 1)
+    pl.semaphore_wait(barrier, groups - 1 + jnp.minimum(shards - 1 - seq, 1))
     for step in range(1, groups):
         share(step).start()
 
@@ -493,13 +495,14 @@
     chunks = part.shape[1] // CHUNK
     per = chunks // groups
     copies = []
-    for chunk in range(chunks):
-        columns = pl.ds(chunk * CHUNK, CHUNK)
-        if chunk % per < per - 1:
-            copies.append(
-                pltpu.make_async_copy(part.at[:, columns], o_hbm.at[:, columns], sem.at[chunk])
-            )
-            copies[-1].start()
+    half = part.shape[0] // 2
+    for piece in range(2 * groups if per > 1 else 0):
+        columns = pl.ds(piece // 2 * per * CHUNK, (per - 1) * CHUNK)
+        where = (pl.ds(piece % 2 * half, half), columns)
+        copies.append(
+            pltpu.make_async_copy(part.at[where], o_hbm.at[where], sem.at[groups + piece])
+        )
+        copies[-1].start()
     for owner in range(groups):
         chunk = owner * per + per - 1
         columns = pl.ds(chunk * CHUNK, CHUNK)
@@ -507,7 +510,7 @@
         growth = mm(grow[...], expander(chunk, 2 * LANES, CHUNK // head_dim, head_dim))
         ready[owner] = part[:, columns] + carried * growth
         copies.append(
-            pltpu.make_async_copy(ready.at[owner], o_hbm.at[:, columns], sem.at[chunk])
+            pltpu.make_async_copy(ready.at[owner], o_hbm.at[:, columns], sem.at[owner])
         )
         copies[-1].start()
     for copy in copies:
@@ -578,7 +581,7 @@
         out_shape=jax.ShapeDtypeStruct((tokens, width), f32),
         in_specs=[vmem] * 4,
         out_specs=pl.BlockSpec(memory_space=pl.ANY),
-        scratch_shapes=[pltpu.VMEM((groups, tokens, CHUNK), f32), dma((chunks,))],
+        scratch_shapes=[pltpu.VMEM((groups, tokens, CHUNK), f32), dma((3 * groups,))],
         compiler_params=pltpu.CompilerParams(vmem_limit_bytes=16 << 20),
     )(*parts)
 

time: 66.9 us -> 66.7 us (level)
  no operation moved by 1% of the time
where the time goes in v6:
time: 66.7 us; the launch traced here: 66.6 us
  Pallas kernels  66.6 us (100%)
    pallas_call x1, Pallas kernels, in_one(): pl.pallas_call(functools.partial(whole_kernel, groups, shards, head_dim),...  64.2 us
    pallas_call x1, Pallas kernels, in_one(): pl.pallas_call(functools.partial(closing_kernel, groups, head_dim), out_s...  2.43 us

profile of v6, /device:TPU:0, one launch (start us, length us, event | category | flops | bytes accessed | tf_op | source)
XLA Modules:
  0.0 66.6 jit_solution(7453599197655259223)
XLA Ops:
  0.0 64.2 %shard_map.55 = (f32[256,5120]{1,0:T(8,128)S(1)}, f32[4,128,256]{2,1,0:T(8,128)S(1)}, bf16[256,256]{1,0:T(8,128)(2,1)S(1)}, bf16[256,384]{1,0:T(8,128)(2,1)S(1)}) custom-call(f32[256,5120]{1,0:T(8,128)} %x_hbm.1, f32[80,256]{1,0:T(8,128)} %bitcast.2, f32[256,128]{1,0:T(8,128)} %b_hbm.1, f32[256,128]{1,0:T(8,128)} %c_hbm.1, f32[1,80]{1,0:T(1,128)} %bitcast.3), custom_call_target="tpu_custom_call" | custom-call | tf_op jit(solution)/shard_map/pallas_call | solution.py:530
  64.2 2.4 %shard_map.56 = f32[256,5120]{1,0:T(8,128)} custom-call(f32[256,5120]{1,0:T(8,128)S(1)} %get-tuple-element.9.part, f32[4,128,256]{2,1,0:T(8,128)S(1)} %get-tuple-element.10.late, bf16[256,256]{1,0:T(8,128)(2,1)S(1)} %get-tuple-element.11.grow, bf16[256,384]{1,0:T(8,128)(2,1)S(1)} %get-tuple-element.12.readout), custom_call_target="tpu_custom_call" | custom-call | tf_op jit(solution)/shard_map/pallas_call | solution.py:579
